TPU v7x, 32 devices: a whole 2x2x4 slice. The times are simulated.
32 devices in a mesh: gauss: 16 (over z, x, core), tile: 2 (over y).
Axes of the slice: x: 2, y: 2, z: 4, core: 2. Of those that a mesh axis runs over, the one named last changes fastest.
Arguments:
- splats: float32 [9, 32768], P(None, ('gauss', 'tile')), may hold values from -8 to 260, as said below
- sh_coeffs: float32 [48, 32768], P(None, ('gauss', 'tile')), may hold values from -2 to 2
- send_list: int32 [32768], P(('gauss', 'tile')), may hold values from 0 to 1023, as said below
- block_slots: int32 [16, 96, 128], P('gauss', 'tile'), may hold values from 0 to 1023, as said below
- block_tiles: int32 [16, 96], P('gauss', 'tile'), may hold values from 0 to 8, as said below
- target: float32 [3, 256, 256], P(None, 'gauss', 'tile'), may hold values from 0 to 1
Outputs:
- rendered: float32 [3, 256, 256], P(None, 'gauss', 'tile')
- grad_splats: float32 [9, 32768], P(None, ('gauss', 'tile'))
- grad_sh: float32 [48, 32768], P(None, ('gauss', 'tile'))
Inputs may be any that keep to these rules, and one draw needn't show every extreme that they name: `send_list`: each device's 1024 entries are a permutation of 0 to 1023. `block_tiles`: each device's 48 entries never fall; each of its tiles 0 to 7 has at least one block; the value 8 marks an unused slot; in every draw some device uses all 48 slots. `block_slots`: entries index the device's received Gaussians. `splats`: conics are positive definite; view directions have unit length; opacity logits (row 5) lie between -8 and -2.
All inputs are finite; a program needn't handle non-finite values.
Results may differ from a plain program's by a relative error of at most 0.0003.
Values sent between devices are 32-bit elements; how exact they have to be, the bound alone decides.
A program may use at most 64 MiB of HBM per device.

v0:
```python
import jax
import jax.numpy as jnp
from jax import lax
from jax.sharding import PartitionSpec as P

TILE_SIDE = 16
TILES_DEV = 8
HIGHEST = lax.Precision.HIGHEST
BASE_ZERO = 0.28209479177387814
BASE_ONE = 0.4886025119029199
BASE_TWO = (
    1.0925484305920792,
    -1.0925484305920792,
    0.31539156525252005,
    -1.0925484305920792,
    0.5462742152960396,
)
BASE_THREE = (
    -0.5900435899266435,
    2.890611442640554,
    -0.4570457994644658,
    0.3731763325901154,
    -0.4570457994644658,
    1.445305721320277,
    -0.5900435899266435,
)
CONST_ONE = 0.0001
CONST_TWO = 0.0009


def extended(cells, sides, width):
    for axis, dim in sides:
        count = lax.axis_size(axis)
        ends = count - 1
        head = lax.slice_in_dim(cells, 0, width, axis=dim)
        tail = lax.slice_in_dim(cells, cells.shape[dim] - width, cells.shape[dim], axis=dim)
        cells = jnp.concatenate(
            [
                lax.ppermute(tail, axis, [(i, (i + 1) % count) for i in range(ends)]),
                cells,
                lax.ppermute(head, axis, [((i + 1) % count, i) for i in range(ends)]),
            ],
            axis=dim,
        )
    return cells


def harmonics(direction):
    coord_x, coord_y, coord_z = (direction[0], direction[1], direction[2])
    square_x, square_y, square_z = (coord_x * coord_x, coord_y * coord_y, coord_z * coord_z)
    rows_list = [
        jnp.full_like(coord_x, BASE_ZERO),
        -BASE_ONE * coord_y,
        BASE_ONE * coord_z,
        -BASE_ONE * coord_x,
        BASE_TWO[0] * coord_x * coord_y,
        BASE_TWO[1] * coord_y * coord_z,
        BASE_TWO[2] * (2.0 * square_z - square_x - square_y),
        BASE_TWO[3] * coord_x * coord_z,
        BASE_TWO[4] * (square_x - square_y),
        BASE_THREE[0] * coord_y * (3.0 * square_x - square_y),
        BASE_THREE[1] * coord_x * coord_y * coord_z,
        BASE_THREE[2] * coord_y * (4.0 * square_z - square_x - square_y),
        BASE_THREE[3] * coord_z * (2.0 * square_z - 3.0 * square_x - 3.0 * square_y),
        BASE_THREE[4] * coord_x * (4.0 * square_z - square_x - square_y),
        BASE_THREE[5] * coord_z * (square_x - square_y),
        BASE_THREE[6] * coord_x * (square_x - 3.0 * square_y),
    ]
    return jnp.stack(rows_list)


def shade(direction, coeffs):
    basis = harmonics(direction)
    return 0.5 + jnp.sum(coeffs.reshape(3, 16, -1) * basis[None], axis=1)


def composite(records):
    members = records.shape[1]
    pixels = jnp.arange(TILE_SIDE * TILE_SIDE)
    pixel_u = (pixels % TILE_SIDE).astype(jnp.float32)
    pixel_v = (pixels // TILE_SIDE).astype(jnp.float32)
    delta_x = pixel_u[None, :] - records[0][:, None]
    delta_y = pixel_v[None, :] - records[1][:, None]
    exponent = (
        -0.5 * (records[2][:, None] * delta_x * delta_x + records[4][:, None] * delta_y * delta_y)
        - records[3][:, None] * delta_x * delta_y
    )
    alphas = jax.nn.sigmoid(records[5])[:, None] * jnp.exp(exponent)
    logged = jnp.log1p(-alphas)
    positions = jnp.arange(members)
    earlier_mask = (positions[None, :] < positions[:, None]).astype(jnp.float32)
    before = jnp.dot(earlier_mask, logged, precision=HIGHEST, preferred_element_type=jnp.float32)
    weight = alphas * jnp.exp(before)
    colour = jnp.dot(records[6:9], weight, precision=HIGHEST, preferred_element_type=jnp.float32)
    return jnp.concatenate([colour, jnp.sum(logged, axis=0, keepdims=True)], axis=0)


def block_pullback(paired):
    unused, pulling = jax.vjp(composite, paired[0])
    return pulling(paired[1])[0]


def combine(results, tile_ids):
    positions = jnp.arange(results.shape[0])
    earlier = (
        (tile_ids[:, None] == tile_ids[None, :]) & (positions[None, :] < positions[:, None])
    ).astype(jnp.float32)
    prefix = jnp.dot(earlier, results[:, 3], precision=HIGHEST, preferred_element_type=jnp.float32)
    member = (jnp.arange(TILES_DEV)[:, None] == tile_ids[None, :]).astype(jnp.float32)
    shaded = jnp.exp(prefix)[:, None, :] * results[:, 0:3]
    return jnp.einsum("kb,bcp->kcp", member, shaded, precision=HIGHEST)


def to_image(tiles_img):
    return (
        tiles_img.reshape(TILES_DEV, 3, TILE_SIDE, TILE_SIDE)
        .transpose(1, 2, 0, 3)
        .reshape(3, TILE_SIDE, TILES_DEV * TILE_SIDE)
    )


def window():
    tap_offsets = jnp.arange(11).astype(jnp.float32) - 5.0
    profile = jnp.exp(-tap_offsets * tap_offsets / 4.5)
    return profile / jnp.sum(profile)


def blur(padded, rows_out, cols_out):
    weights = window()
    across = weights[0] * padded[..., :, 0:cols_out]
    for offset in range(1, 11):
        across = across + weights[offset] * padded[..., :, offset : offset + cols_out]
    result = weights[0] * across[..., 0:rows_out, :]
    for offset in range(1, 11):
        result = result + weights[offset] * across[..., offset : offset + rows_out, :]
    return result


def similarity(mu_x, mu_y, sq_x, sq_y, cross_xy):
    mean_xy = mu_x * mu_y
    numerator = (2.0 * mean_xy + CONST_ONE) * (2.0 * (cross_xy - mean_xy) + CONST_TWO)
    denominator = (mu_x * mu_x + mu_y * mu_y + CONST_ONE) * (
        sq_x - mu_x * mu_x + sq_y - mu_y * mu_y + CONST_TWO
    )
    return numerator / denominator


def five_products(padded):
    return jnp.stack(
        [padded[0], padded[1], padded[0] * padded[0], padded[1] * padded[1], padded[0] * padded[1]]
    )


def similarity_grads(moments):

    def partial_loss(mean_x, square_x, product_xy):
        return jnp.sum(
            0.2 * (1.0 - similarity(mean_x, moments[1], square_x, moments[3], product_xy))
        )

    return jnp.stack(jax.grad(partial_loss, argnums=(0, 1, 2))(moments[0], moments[2], moments[4]))


def run_live(apply, arrays_in, live, out_shape):

    def advance(position, buffer):
        picked = tuple(
            (lax.dynamic_index_in_dim(member, position, 0, keepdims=False) for member in arrays_in)
        )
        return lax.dynamic_update_index_in_dim(buffer, apply(picked), position, 0)

    return lax.fori_loop(0, live, advance, jnp.zeros(out_shape, jnp.float32))


def body(splats, sh_coeffs, send_list, block_slots, block_tiles, target):
    row_band = lax.axis_index("gauss")
    col_band = lax.axis_index("tile")
    owners = lax.axis_size("gauss")
    peers = lax.axis_size("tile")
    own_records = jnp.concatenate([splats[0:6], shade(splats[6:9], sh_coeffs)], axis=0)
    received = lax.all_to_all(
        own_records[:, send_list], "gauss", split_axis=1, concat_axis=1, tiled=True
    )
    tile_ids = block_tiles[0]
    slot_rows = block_slots[0]
    slots_total = slot_rows.shape[0]
    gathered = received[:, slot_rows.reshape(-1)].reshape(9, slots_total, slot_rows.shape[1])
    anchor_x = (TILE_SIDE * (TILES_DEV * col_band + jnp.minimum(tile_ids, TILES_DEV - 1))).astype(
        jnp.float32
    )
    anchor_y = (TILE_SIDE * row_band).astype(jnp.float32)
    shifted = jnp.concatenate(
        [gathered[0:1] - anchor_x[None, :, None], gathered[1:2] - anchor_y, gathered[2:9]], axis=0
    )
    per_block = jnp.moveaxis(shifted, 1, 0)
    live = jnp.sum((tile_ids < TILES_DEV).astype(jnp.int32))
    pixel_count = TILE_SIDE * TILE_SIDE
    results = run_live(
        lambda picked: composite(picked[0]), (per_block,), live, (slots_total, 4, pixel_count)
    )
    tiles_img = combine(results, tile_ids)
    rendered = to_image(tiles_img)
    rows_here = rendered.shape[1]
    cols_here = rendered.shape[2]
    padded = extended(jnp.stack([rendered, target]), (("gauss", 2), ("tile", 3)), 10)
    moments = blur(five_products(padded), rows_here + 10, cols_here + 10)
    grads_map = similarity_grads(moments)
    row_ids = row_band * rows_here - 5 + jnp.arange(rows_here + 10)
    col_ids = col_band * cols_here - 5 + jnp.arange(cols_here + 10)
    inside = ((row_ids >= 0) & (row_ids < rows_here * owners))[:, None] & (
        (col_ids >= 0) & (col_ids < cols_here * peers)
    )[None, :]
    spread = blur(grads_map * inside.astype(jnp.float32), rows_here, cols_here)
    pixel_grad = (
        spread[0] + 2.0 * rendered * spread[1] + target * spread[2] + 1.6 * (rendered - target)
    )
    tile_grad = (
        pixel_grad.reshape(3, TILE_SIDE, TILES_DEV, TILE_SIDE)
        .transpose(2, 0, 1, 3)
        .reshape(TILES_DEV, 3, pixel_count)
    )
    unused, combine_pull = jax.vjp(lambda found: combine(found, tile_ids), results)
    results_grad = combine_pull(tile_grad)[0]
    block_grad = run_live(block_pullback, (per_block, results_grad), live, per_block.shape)
    flat_grad = jnp.moveaxis(block_grad, 0, 1).reshape(9, -1)
    table_grad = jnp.zeros_like(received).at[:, slot_rows.reshape(-1)].add(flat_grad)
    back_records = lax.all_to_all(table_grad, "gauss", split_axis=1, concat_axis=1, tiled=True)
    own_grad = jnp.zeros_like(own_records).at[:, send_list].set(back_records)
    unused_colour, shade_pull = jax.vjp(shade, splats[6:9], sh_coeffs)
    dir_grad, grad_sh = shade_pull(own_grad[6:9])
    grad_splats = jnp.concatenate([own_grad[0:6], dir_grad], axis=0)
    return (rendered, grad_splats, grad_sh)


def solution(mesh):
    in_specs = (
        P(None, ("gauss", "tile")),
        P(None, ("gauss", "tile")),
        P(("gauss", "tile")),
        P("gauss", "tile", None),
        P("gauss", "tile"),
        P(None, "gauss", "tile"),
    )
    out_specs = (P(None, "gauss", "tile"), P(None, ("gauss", "tile")), P(None, ("gauss", "tile")))
    return jax.shard_map(body, mesh=mesh, in_specs=in_specs, out_specs=out_specs, check_vma=False)
```

profile of v0, /device:TPU:0, one launch (start us, length us, event | category | flops | bytes accessed | tf_op | source)
XLA Modules:
  0.0 363.7 jit_solution(15220192069105559157)
XLA Ops:
  0.6 0.9 multiply_multiply_fusion.2
  1.5 0.8 slice.409
  2.3 0.9 multiply_multiply_fusion.3
  3.3 1.0 multiply_reduce_fusion.2
  5.3 2.8 gather_fusion
  9.0 7.4 %all-to-all-start = ((f32[16,1,576]{2,1,0:T(1,128)}), f32[16,1,576]{2,1,0:T(1,128)S(1)}, u32[]{:S(2)}, u32[]{:S(2)}) async-start(f32[16,1,576]{2,1,0:T(1,128)} %reshape.453), calls=%async_computation | async-start | bytes 81920 | tf_op jit(solution)/shard_map/all_to_all | solution.py:181
  16.4 0.8 compare_select_fusion
  17.3 1.4 multiply_convert_fusion
  19.3 3.8 %all-to-all-done = f32[16,1,576]{2,1,0:T(1,128)S(1)} async-done(((f32[16,1,576]{2,1,0:T(1,128)}), f32[16,1,576]{2,1,0:T(1,128)S(1)}, u32[]{:S(2)}, u32[]{:S(2)}) %all-to-all-start) | async-done | bytes 36896 | tf_op jit(solution)/shard_map/all_to_all | solution.py:181
  24.5 1.0 copy.59
  25.5 17.1 %gather_fusion.1 = f32[6144,9]{1,0:T(8,128)S(1)} fusion(f32[9,1024]{0,1:T(8,128)} %bitcast.194, s32[6144]{0:T(1024)S(1)} %broadcast_clamp_fusion), kind=kCustom, calls=%fused_computation.1 | custom fusion | bytes 466944 | tf_op jit(solution)/shard_map/gather | solution.py:187
  42.6 2.5 slice.497
  45.2 2.5 slice_reduce_fusion
  47.7 2.4 copy.62
  50.3 24.7 %while.24 = (s32[]{:T(128)}, f32[48,4,256]{2,1,0:T(4,128)S(1)}, s32[]{:T(128)}, f32[48,9,128]{2,1,0:T(8,128)S(1)}, s32[]{:T(128)}, /*index=5*/s32[]{:T(128)}, s3...) while((s32[]{:T(128)}, f32[48,4,256]{2,1,0:T(4,128)S(1)}, s32[]{:T(128)}, f32[48,9,128]{2,1,0:T(8,128)S(1)}, ...), condition=%wide.region_4.5_spmd, body=%wide.region_2.4_spmd.sunk | while | flops 52843144 | bytes 296203 | solution.py:172
  75.9 54.4 %collective-permute-start = (f32[2,3,10,128]{3,2,1,0:T(8,128)S(1)}, f32[2,3,10,128]{3,2,1,0:T(8,128)S(1)}, u32[]{:S(2)}, u32[]{:S(2)}) collective-permute-start(f32[2,3,10,128]{3,2,1,0:T(8,128)S(1)} %get-tuple-element.234), channel_id=1, source_target_pairs={{0,2},{2,4},{4,6},{6,8},{8,10},{10,12},{12,14},{14,16},{16,18},{18... | collective-permute-start | bytes 92168 | tf_op jit(solution)/shard_map/ppermute | solution.py:39
  130.2 1.3 collective-permute-start.1
  132.1 1.5 collective-permute-done.1
  133.7 2.9 collective-permute-start.2
  136.7 1.3 collective-permute-start.3
  138.8 1.1 collective-permute-done.2
  139.9 4.7 %collective-permute-done.3 = f32[2,3,36,10]{3,2,1,0:T(8,128)S(1)} collective-permute-done((f32[2,3,36,10]{3,2,1,0:T(8,128)S(1)}, f32[2,3,36,10]{3,2,1,0:T(8,128)S(1)}, u32[]{:S(2)}, u32[]{:S(2)}) %collective-permute-start.3) | collective-permute-done | bytes 8672 | tf_op jit(solution)/shard_map/ppermute | solution.py:41
  145.0 8.4 %fusion.74 = f32[5,3,36,138]{3,2,1,0:T(8,128)S(1)} fusion(f32[5,3,36,148]{3,2,1,0:T(8,128)S(1)} %pad_maximum_fusion, f32[]{:T(128)} %bitcast.51, f32[]{:T(128)} %bitcast.50, f32[]{:T(128)} %bitcast.49, f32[]{:T(128)} %bitcast.48, f32[]{:T(128)} %bitcast.47, f32[]{:T(128)} %bitcast.46, f32[]{:T(128)} %bitcast.45, f32[]{:T(128)} %bitcast.44, f32[]{:T(128)} %bitcast.43, ...), kind=kLoop, calls=%fused_computation.138 | loop fusion | flops 1564920 | bytes 3577004 | tf_op jit(solution)/shard_map/add | solution.py:132
  153.4 7.4 %fusion.84 = f32[5,3,26,138]{3,2,1,0:T(8,128)S(1)} fusion(f32[5,3,36,138]{3,2,1,0:T(8,128)S(1)} %fusion.74, f32[]{:T(128)} %bitcast.51, f32[]{:T(128)} %bitcast.50, f32[]{:T(128)} %bitcast.49, f32[]{:T(128)} %bitcast.48, f32[]{:T(128)} %bitcast.47, f32[]{:T(128)} %bitcast.46, f32[]{:T(128)} %bitcast.45, f32[]{:T(128)} %bitcast.44, f32[]{:T(128)} %bitcast.43, ...), kind=kLoop, calls=%fused_computation.160 | loop fusion | flops 1130220 | bytes 2583404 | tf_op jit(solution)/shard_map/add | solution.py:135
  161.1 7.2 %fusion.98 = f32[3,3,26,128]{3,2,1,0:T(8,128)S(1)} fusion(f32[3,3,26,138]{3,2,1,0:T(8,128)S(1)} %maximum_multiply_fusion, f32[]{:T(128)} %bitcast.51, f32[]{:T(128)} %bitcast.50, f32[]{:T(128)} %bitcast.49, f32[]{:T(128)} %bitcast.48, f32[]{:T(128)} %bitcast.47, f32[]{:T(128)} %bitcast.46, f32[]{:T(128)} %bitcast.45, f32[]{:T(128)} %bitcast.44, ...), kind=kLoop, calls=%fused_computation.193 | loop fusion | flops 628992 | bytes 1437740 | tf_op jit(solution)/shard_map/add | solution.py:132
  168.3 6.9 %fusion.117 = f32[3,3,16,128]{3,2,1,0:T(8,128)S(1)} fusion(f32[3,3,26,128]{3,2,1,0:T(8,128)S(1)} %fusion.98, f32[]{:T(128)} %bitcast.51, f32[]{:T(128)} %bitcast.50, f32[]{:T(128)} %bitcast.49, f32[]{:T(128)} %bitcast.48, f32[]{:T(128)} %bitcast.47, f32[]{:T(128)} %bitcast.46, f32[]{:T(128)} %bitcast.45, f32[]{:T(128)} %bitcast.44, f32[]{:T(128)} %bitcast.43, ...), kind=kLoop, calls=%fused_computation.238 | loop fusion | flops 387072 | bytes 884780 | tf_op jit(solution)/shard_map/add | solution.py:135
  176.1 43.1 %while.25 = (s32[]{:T(128)}, f32[48,9,128]{2,1,0:T(8,128)S(1)}, s32[]{:T(128)}, f32[48,4,256]{2,0,1:T(8,128)S(1)}, f32[48,9,128]{2,1,0:T(8,128)S(1)}, /*index=5*...) while((s32[]{:T(128)}, f32[48,9,128]{2,1,0:T(8,128)S(1)}, ...), condition=%wide.region_14.15_spmd, body=%wide.region_7.0_spmd.sunk | while | flops 106244616 | bytes 1247007 | solution.py:172
  219.5 1.1 copy.69
  220.6 34.3 %scatter_custom_fusion = f32[9,1024]{0,1:T(8,128)} fusion(s32[6144]{0:T(1024)} %bitcast.222, f32[6144,9]{1,0:T(8,128)S(1)} %copy.69, f32[]{:T(128)} %constant.207.clone.1), kind=kCustom, calls=%fused_computation.184 | custom fusion | flops 55296 | bytes 37376 | tf_op jit(solution)/shard_map/scatter-add | solution.py:226
  254.8 1.3 copy.70
  256.2 100.8 %all_to_all.24 = f32[16,1,576]{2,1,0:T(1,128)S(1)} all-to-all(f32[16,1,576]{2,1,0:T(1,128)S(1)} %reshape.455), channel_id=1, replica_groups=mesh['gauss'=16,'tile'=2] {'gauss'}, dimensions={0} | all-to-all | bytes 73728 | tf_op jit(solution)/shard_map/all_to_all | solution.py:227
  358.2 3.2 scatter_custom_fusion.1
  (366 shorter events, 55.1 us)
Async XLA Ops:
  3.3 1.0 copy-start.2
  9.0 14.1 %all-to-all-start = ((f32[16,1,576]{2,1,0:T(1,128)}), f32[16,1,576]{2,1,0:T(1,128)S(1)}, u32[]{:S(2)}, u32[]{:S(2)}) async-start(f32[16,1,576]{2,1,0:T(1,128)} %reshape.453), calls=%async_computation | async-start | bytes 81920 | tf_op jit(solution)/shard_map/all_to_all | solution.py:181
  17.2 6.4 %copy-start.6 = (s32[6144,1]{0,1:T(1,128)}, s32[6144,1]{0,1:T(1,128)S(1)}, u32[]{:S(2)}) copy-start(s32[6144,1]{0,1:T(1,128)S(1)} %compare_select_fusion) | copy-start | bytes 73732
  50.3 24.8 %copy-start.7 = (s32[1,48]{1,0:T(1,128)S(1)}, s32[1,48]{1,0:T(1,128)}, u32[]{:S(2)}) copy-start(s32[1,48]{1,0:T(1,128)} %param.14) | copy-start | bytes 580
  50.3 25.6 %copy-start.1 = (f32[3,16,128]{2,1,0:T(8,128)S(1)}, f32[3,16,128]{2,1,0:T(8,128)}, u32[]{:S(2)}) copy-start(f32[3,16,128]{2,1,0:T(8,128)} %param.15) | copy-start | bytes 73732
  75.9 56.3 %collective-permute-start = (f32[2,3,10,128]{3,2,1,0:T(8,128)S(1)}, f32[2,3,10,128]{3,2,1,0:T(8,128)S(1)}, u32[]{:S(2)}, u32[]{:S(2)}) collective-permute-start(f32[2,3,10,128]{3,2,1,0:T(8,128)S(1)} %get-tuple-element.234), channel_id=1, source_target_pairs={{0,2},{2,4},{4,6},{6,8},{8,10},{10,12},{12,14},{14,16},{16,18},{18... | collective-permute-start | bytes 92168 | tf_op jit(solution)/shard_map/ppermute | solution.py:39
  130.2 3.4 collective-permute-start.1
  133.7 6.1 %collective-permute-start.2 = (f32[2,3,36,10]{3,2,1,0:T(8,128)S(1)}, f32[2,3,36,10]{3,2,1,0:T(8,128)S(1)}, u32[]{:S(2)}, u32[]{:S(2)}) collective-permute-start(f32[2,3,36,10]{3,2,1,0:T(8,128)S(1)} %get-tuple-element.216), channel_id=1, source_target_pairs={{0,1},{2,3},{4,5},{6,7},{8,9},{10,11},{12,13},{14,15},{16,17},{18,... | collective-permute-start | bytes 25928 | tf_op jit(solution)/shard_map/ppermute | solution.py:39
  136.7 7.9 %collective-permute-start.3 = (f32[2,3,36,10]{3,2,1,0:T(8,128)S(1)}, f32[2,3,36,10]{3,2,1,0:T(8,128)S(1)}, u32[]{:S(2)}, u32[]{:S(2)}) collective-permute-start(f32[2,3,36,10]{3,2,1,0:T(8,128)S(1)} %get-tuple-element.217), channel_id=1, source_target_pairs={{1,0},{3,2},{5,4},{7,6},{9,8},{11,10},{13,12},{15,14},{17,16},{19,... | collective-permute-start | bytes 25928 | tf_op jit(solution)/shard_map/ppermute | solution.py:41
  138.8 36.4 %copy-start.5 = (f32[3,16,128]{2,1,0:T(8,128)}, f32[3,16,128]{2,1,0:T(8,128)S(1)}, u32[]{:S(2)}) copy-start(f32[3,16,128]{2,1,0:T(8,128)S(1)} %reshape.407) | copy-start | bytes 73732
  220.5 141.3 %copy-start = (f32[48,1024]{1,0:T(8,128)S(1)}, f32[48,1024]{1,0:T(8,128)}, u32[]{:S(2)}) copy-start(f32[48,1024]{1,0:T(8,128)} %param.11) | copy-start | bytes 589828
  220.5 141.3 %copy-start.3 = (f32[16,1024]{1,0:T(8,128)S(1)}, f32[16,1024]{1,0:T(8,128)}, u32[]{:S(2)}) copy-start(f32[16,1024]{1,0:T(8,128)} %copy-done.2) | copy-start | bytes 196612
  220.5 142.0 %copy-start.4 = (f32[9,1024]{1,0:T(8,128)S(1)}, f32[9,1024]{1,0:T(8,128)}, u32[]{:S(2)}) copy-start(f32[9,1024]{1,0:T(8,128)} %param.10) | copy-start | bytes 110596
where the time goes:
time: 366 us; the launch traced here: 364 us
  blocking collectives  101 us (28%)
  other arithmetic  89.2 us (24%)
  starting transfers between devices  67.2 us (18%)
  local copies, waits for them, and re-layouts  37.4 us (10%)
  matrix products  32.3 us (9%)
  loops' own time  24.5 us (7%)
  waiting for transfers between devices  11 us (3%)
    all_to_all x1, blocking collectives, body(): lax.all_to_all(table_grad, 'gauss', split_axis=1, concat_axis=1, tiled=True)  101 us
    ppermute x2, starting transfers between devices, extended(): lax.ppermute(tail, axis, [(i, (i + 1) % count) for i in range(ends)])  57.3 us
    scatter-add x1, other arithmetic, body(): jnp.zeros_like(received).at[:, slot_rows.reshape(-1)].add(flat_grad)  34.3 us
    another operation x2, loops' own time, run_live(): return lax.fori_loop(0, live, advance, jnp.zeros(out_shape, jnp.float32))  24.5 us
    dot_general x45, matrix products, composite(): jnp.dot(earlier_mask, logged, precision=HIGHEST, preferred_element_type=j...  19.3 us
    gather x1, local copies, waits for them, and re-layouts, body(): received[:, slot_rows.reshape(-1)]  17.1 us
    add x2, other arithmetic, blur(): across = across + weights[offset] * padded[..., :, offset:offset + cols_out]  15.7 us
    add x2, other arithmetic, blur(): result = result + weights[offset] * across[..., offset:offset + rows_out, :]  14.3 us
  transfers between devices with their start and end apart: 5, of which 4 were waited for; matrix products, arithmetic and copies ran while one was open for 1% of the time, Pallas kernels for 0%

commit v1 on v0

--- a/solution.py
+++ b/solution.py
@@ -224,7 +224,12 @@
     block_grad = run_live(block_pullback, (per_block, results_grad), live, per_block.shape)
     flat_grad = jnp.moveaxis(block_grad, 0, 1).reshape(9, -1)
     table_grad = jnp.zeros_like(received).at[:, slot_rows.reshape(-1)].add(flat_grad)
-    back_records = lax.all_to_all(table_grad, "gauss", split_axis=1, concat_axis=1, tiled=True)
+    back_records = jnp.concatenate(
+        lax.all_to_all(
+            jnp.stack(jnp.split(table_grad, lax.axis_size("gauss"), axis=1)), "gauss", 0, 0
+        ),
+        axis=1,
+    )
     own_grad = jnp.zeros_like(own_records).at[:, send_list].set(back_records)
     unused_colour, shade_pull = jax.vjp(shade, splats[6:9], sh_coeffs)
     dir_grad, grad_sh = shade_pull(own_grad[6:9])

time: 366 us -> 378 us (1.033)
  local copies, waits for them, and re-layouts: 37.4 us -> 48.5 us
    unnamed x22 -> x37, local copies, waits for them, and re-layouts: 1.2 us -> 12.6 us
where the time goes in v1:
time: 378 us; the launch traced here: 375 us
  blocking collectives  101 us (27%)
  other arithmetic  89.2 us (24%)
  starting transfers between devices  67.2 us (18%)
  local copies, waits for them, and re-layouts  48.5 us (13%)
  matrix products  32.3 us (9%)
  loops' own time  24.5 us (6%)
  waiting for transfers between devices  11 us (3%)
    all_to_all x1, blocking collectives, body(): lax.all_to_all(jnp.stack(jnp.split(table_grad, lax.axis_size('gauss'), ax...  101 us
    ppermute x2, starting transfers between devices, extended(): lax.ppermute(tail, axis, [(i, (i + 1) % count) for i in range(ends)])  57.3 us
    scatter-add x1, other arithmetic, body(): jnp.zeros_like(received).at[:, slot_rows.reshape(-1)].add(flat_grad)  34.3 us
    another operation x2, loops' own time, run_live(): return lax.fori_loop(0, live, advance, jnp.zeros(out_shape, jnp.float32))  24.5 us
    dot_general x45, matrix products, composite(): jnp.dot(earlier_mask, logged, precision=HIGHEST, preferred_element_type=j...  19.3 us
    gather x1, local copies, waits for them, and re-layouts, body(): received[:, slot_rows.reshape(-1)]  17.1 us
    add x2, other arithmetic, blur(): across = across + weights[offset] * padded[..., :, offset:offset + cols_out]  15.7 us
    add x2, other arithmetic, blur(): result = result + weights[offset] * across[..., offset:offset + rows_out, :]  14.3 us
  transfers between devices with their start and end apart: 5, of which 4 were waited for; matrix products, arithmetic and copies ran while one was open for 1% of the time, Pallas kernels for 0%

profile of v1, /device:TPU:0, one launch (start us, length us, event | category | flops | bytes accessed | tf_op | source)
XLA Modules:
  0.0 374.8 jit_solution(17849110398606948401)
XLA Ops:
  0.6 0.9 multiply_multiply_fusion.2
  1.5 0.8 slice.409
  2.3 0.9 multiply_multiply_fusion.3
  3.3 1.0 multiply_reduce_fusion.2
  5.3 2.8 gather_fusion
  9.0 7.4 %all-to-all-start = ((f32[16,1,576]{2,1,0:T(1,128)}), f32[16,1,576]{2,1,0:T(1,128)S(1)}, u32[]{:S(2)}, u32[]{:S(2)}) async-start(f32[16,1,576]{2,1,0:T(1,128)} %reshape.459), calls=%async_computation | async-start | bytes 81920 | tf_op jit(solution)/shard_map/all_to_all | solution.py:181
  16.4 0.8 compare_select_fusion
  17.3 1.4 multiply_convert_fusion
  19.3 3.8 %all-to-all-done = f32[16,1,576]{2,1,0:T(1,128)S(1)} async-done(((f32[16,1,576]{2,1,0:T(1,128)}), f32[16,1,576]{2,1,0:T(1,128)S(1)}, u32[]{:S(2)}, u32[]{:S(2)}) %all-to-all-start) | async-done | bytes 36896 | tf_op jit(solution)/shard_map/all_to_all | solution.py:181
  24.5 1.0 copy.109
  25.5 17.1 %gather_fusion.1 = f32[6144,9]{1,0:T(8,128)S(1)} fusion(f32[9,1024]{0,1:T(8,128)} %bitcast.256, s32[6144]{0:T(1024)S(1)} %broadcast_clamp_fusion), kind=kCustom, calls=%fused_computation.1 | custom fusion | bytes 466944 | tf_op jit(solution)/shard_map/gather | solution.py:187
  42.6 2.5 slice.497
  45.2 2.5 slice_reduce_fusion
  47.7 2.4 copy.112
  50.3 24.7 %while.24 = (s32[]{:T(128)}, f32[48,4,256]{2,1,0:T(4,128)S(1)}, s32[]{:T(128)}, f32[48,9,128]{2,1,0:T(8,128)S(1)}, s32[]{:T(128)}, /*index=5*/s32[]{:T(128)}, s3...) while((s32[]{:T(128)}, f32[48,4,256]{2,1,0:T(4,128)S(1)}, s32[]{:T(128)}, f32[48,9,128]{2,1,0:T(8,128)S(1)}, ...), condition=%wide.region_4.5_spmd, body=%wide.region_2.4_spmd.sunk | while | flops 52843144 | bytes 296203 | solution.py:172
  75.9 54.4 %collective-permute-start = (f32[2,3,10,128]{3,2,1,0:T(8,128)S(1)}, f32[2,3,10,128]{3,2,1,0:T(8,128)S(1)}, u32[]{:S(2)}, u32[]{:S(2)}) collective-permute-start(f32[2,3,10,128]{3,2,1,0:T(8,128)S(1)} %get-tuple-element.239), channel_id=1, source_target_pairs={{0,2},{2,4},{4,6},{6,8},{8,10},{10,12},{12,14},{14,16},{16,18},{18... | collective-permute-start | bytes 92168 | tf_op jit(solution)/shard_map/ppermute | solution.py:39
  130.2 1.3 collective-permute-start.1
  132.1 1.5 collective-permute-done.1
  133.7 2.9 collective-permute-start.2
  136.7 1.3 collective-permute-start.3
  138.8 1.1 collective-permute-done.2
  139.9 4.7 %collective-permute-done.3 = f32[2,3,36,10]{3,2,1,0:T(8,128)S(1)} collective-permute-done((f32[2,3,36,10]{3,2,1,0:T(8,128)S(1)}, f32[2,3,36,10]{3,2,1,0:T(8,128)S(1)}, u32[]{:S(2)}, u32[]{:S(2)}) %collective-permute-start.3) | collective-permute-done | bytes 8672 | tf_op jit(solution)/shard_map/ppermute | solution.py:41
  145.0 8.4 %fusion.74 = f32[5,3,36,138]{3,2,1,0:T(8,128)S(1)} fusion(f32[5,3,36,148]{3,2,1,0:T(8,128)S(1)} %pad_maximum_fusion, f32[]{:T(128)} %bitcast.51, f32[]{:T(128)} %bitcast.50, f32[]{:T(128)} %bitcast.49, f32[]{:T(128)} %bitcast.48, f32[]{:T(128)} %bitcast.47, f32[]{:T(128)} %bitcast.46, f32[]{:T(128)} %bitcast.45, f32[]{:T(128)} %bitcast.44, f32[]{:T(128)} %bitcast.43, ...), kind=kLoop, calls=%fused_computation.138 | loop fusion | flops 1564920 | bytes 3577004 | tf_op jit(solution)/shard_map/add | solution.py:132
  153.4 7.4 %fusion.84 = f32[5,3,26,138]{3,2,1,0:T(8,128)S(1)} fusion(f32[5,3,36,138]{3,2,1,0:T(8,128)S(1)} %fusion.74, f32[]{:T(128)} %bitcast.51, f32[]{:T(128)} %bitcast.50, f32[]{:T(128)} %bitcast.49, f32[]{:T(128)} %bitcast.48, f32[]{:T(128)} %bitcast.47, f32[]{:T(128)} %bitcast.46, f32[]{:T(128)} %bitcast.45, f32[]{:T(128)} %bitcast.44, f32[]{:T(128)} %bitcast.43, ...), kind=kLoop, calls=%fused_computation.160 | loop fusion | flops 1130220 | bytes 2583404 | tf_op jit(solution)/shard_map/add | solution.py:135
  161.1 7.2 %fusion.98 = f32[3,3,26,128]{3,2,1,0:T(8,128)S(1)} fusion(f32[3,3,26,138]{3,2,1,0:T(8,128)S(1)} %maximum_multiply_fusion, f32[]{:T(128)} %bitcast.51, f32[]{:T(128)} %bitcast.50, f32[]{:T(128)} %bitcast.49, f32[]{:T(128)} %bitcast.48, f32[]{:T(128)} %bitcast.47, f32[]{:T(128)} %bitcast.46, f32[]{:T(128)} %bitcast.45, f32[]{:T(128)} %bitcast.44, ...), kind=kLoop, calls=%fused_computation.193 | loop fusion | flops 628992 | bytes 1437740 | tf_op jit(solution)/shard_map/add | solution.py:132
  168.3 6.9 %fusion.117 = f32[3,3,16,128]{3,2,1,0:T(8,128)S(1)} fusion(f32[3,3,26,128]{3,2,1,0:T(8,128)S(1)} %fusion.98, f32[]{:T(128)} %bitcast.51, f32[]{:T(128)} %bitcast.50, f32[]{:T(128)} %bitcast.49, f32[]{:T(128)} %bitcast.48, f32[]{:T(128)} %bitcast.47, f32[]{:T(128)} %bitcast.46, f32[]{:T(128)} %bitcast.45, f32[]{:T(128)} %bitcast.44, f32[]{:T(128)} %bitcast.43, ...), kind=kLoop, calls=%fused_computation.238 | loop fusion | flops 387072 | bytes 884780 | tf_op jit(solution)/shard_map/add | solution.py:135
  176.1 43.1 %while.25 = (s32[]{:T(128)}, f32[48,9,128]{2,1,0:T(8,128)S(1)}, s32[]{:T(128)}, f32[48,4,256]{2,0,1:T(8,128)S(1)}, f32[48,9,128]{2,1,0:T(8,128)S(1)}, /*index=5*...) while((s32[]{:T(128)}, f32[48,9,128]{2,1,0:T(8,128)S(1)}, ...), condition=%wide.region_14.15_spmd, body=%wide.region_7.0_spmd.sunk | while | flops 106244616 | bytes 1247007 | solution.py:172
  219.5 1.1 copy.119
  220.6 34.3 %scatter_custom_fusion = f32[9,1024]{0,1:T(8,128)} fusion(s32[6144]{0:T(1024)} %bitcast.282, f32[6144,9]{1,0:T(8,128)S(1)} %copy.119, f32[]{:T(128)} %constant.207.clone.1), kind=kCustom, calls=%fused_computation.184 | custom fusion | flops 55296 | bytes 37376 | tf_op jit(solution)/shard_map/scatter-add | solution.py:226
  257.1 0.8 fusion.143
  267.3 100.8 %all_to_all.17 = f32[16,1,576]{2,1,0:T(1,128)S(1)} all-to-all(f32[16,1,576]{2,1,0:T(1,128)S(1)} %reshape.461), channel_id=1, replica_groups=mesh['gauss'=16,'tile'=2] {'gauss'}, dimensions={0} | all-to-all | bytes 73728 | tf_op jit(solution)/shard_map/all_to_all | solution.py:228
  369.3 3.2 scatter_custom_fusion.1
  (382 shorter events, 66.7 us)
Async XLA Ops:
  3.3 1.0 copy-start.2
  9.0 14.1 %all-to-all-start = ((f32[16,1,576]{2,1,0:T(1,128)}), f32[16,1,576]{2,1,0:T(1,128)S(1)}, u32[]{:S(2)}, u32[]{:S(2)}) async-start(f32[16,1,576]{2,1,0:T(1,128)} %reshape.459), calls=%async_computation | async-start | bytes 81920 | tf_op jit(solution)/shard_map/all_to_all | solution.py:181
  17.2 6.4 %copy-start.6 = (s32[6144,1]{0,1:T(1,128)}, s32[6144,1]{0,1:T(1,128)S(1)}, u32[]{:S(2)}) copy-start(s32[6144,1]{0,1:T(1,128)S(1)} %compare_select_fusion) | copy-start | bytes 73732
  50.3 24.8 %copy-start.7 = (s32[1,48]{1,0:T(1,128)S(1)}, s32[1,48]{1,0:T(1,128)}, u32[]{:S(2)}) copy-start(s32[1,48]{1,0:T(1,128)} %param.14) | copy-start | bytes 580
  50.3 25.6 %copy-start.1 = (f32[3,16,128]{2,1,0:T(8,128)S(1)}, f32[3,16,128]{2,1,0:T(8,128)}, u32[]{:S(2)}) copy-start(f32[3,16,128]{2,1,0:T(8,128)} %param.15) | copy-start | bytes 73732
  75.9 56.3 %collective-permute-start = (f32[2,3,10,128]{3,2,1,0:T(8,128)S(1)}, f32[2,3,10,128]{3,2,1,0:T(8,128)S(1)}, u32[]{:S(2)}, u32[]{:S(2)}) collective-permute-start(f32[2,3,10,128]{3,2,1,0:T(8,128)S(1)} %get-tuple-element.239), channel_id=1, source_target_pairs={{0,2},{2,4},{4,6},{6,8},{8,10},{10,12},{12,14},{14,16},{16,18},{18... | collective-permute-start | bytes 92168 | tf_op jit(solution)/shard_map/ppermute | solution.py:39
  130.2 3.4 collective-permute-start.1
  133.7 6.1 %collective-permute-start.2 = (f32[2,3,36,10]{3,2,1,0:T(8,128)S(1)}, f32[2,3,36,10]{3,2,1,0:T(8,128)S(1)}, u32[]{:S(2)}, u32[]{:S(2)}) collective-permute-start(f32[2,3,36,10]{3,2,1,0:T(8,128)S(1)} %get-tuple-element.221), channel_id=1, source_target_pairs={{0,1},{2,3},{4,5},{6,7},{8,9},{10,11},{12,13},{14,15},{16,17},{18,... | collective-permute-start | bytes 25928 | tf_op jit(solution)/shard_map/ppermute | solution.py:39
  136.7 7.9 %collective-permute-start.3 = (f32[2,3,36,10]{3,2,1,0:T(8,128)S(1)}, f32[2,3,36,10]{3,2,1,0:T(8,128)S(1)}, u32[]{:S(2)}, u32[]{:S(2)}) collective-permute-start(f32[2,3,36,10]{3,2,1,0:T(8,128)S(1)} %get-tuple-element.222), channel_id=1, source_target_pairs={{1,0},{3,2},{5,4},{7,6},{9,8},{11,10},{13,12},{15,14},{17,16},{19,... | collective-permute-start | bytes 25928 | tf_op jit(solution)/shard_map/ppermute | solution.py:41
  138.8 36.4 %copy-start.5 = (f32[3,16,128]{2,1,0:T(8,128)}, f32[3,16,128]{2,1,0:T(8,128)S(1)}, u32[]{:S(2)}) copy-start(f32[3,16,128]{2,1,0:T(8,128)S(1)} %reshape.411) | copy-start | bytes 73732
  220.5 152.4 %copy-start = (f32[48,1024]{1,0:T(8,128)S(1)}, f32[48,1024]{1,0:T(8,128)}, u32[]{:S(2)}) copy-start(f32[48,1024]{1,0:T(8,128)} %param.11) | copy-start | bytes 589828
  220.5 152.4 %copy-start.3 = (f32[16,1024]{1,0:T(8,128)S(1)}, f32[16,1024]{1,0:T(8,128)}, u32[]{:S(2)}) copy-start(f32[16,1024]{1,0:T(8,128)} %copy-done.2) | copy-start | bytes 196612
  220.5 153.1 %copy-start.4 = (f32[9,1024]{1,0:T(8,128)S(1)}, f32[9,1024]{1,0:T(8,128)}, u32[]{:S(2)}) copy-start(f32[9,1024]{1,0:T(8,128)} %param.10) | copy-start | bytes 110596
